TPU v7x, 32 devices: a whole 2x2x4 slice. The times are simulated.
32 devices in a mesh: dp: 16 (over z, y, x), mp: 2 (over core).
Axes of the slice: x: 2, y: 2, z: 4, core: 2. Of those that a mesh axis runs over, the one named last changes fastest.
Arguments:
- inputs: bfloat16 [32768, 4096], P('dp', 'mp'), may hold values from -6 to 6
- cotangents: bfloat16 [32768, 4096], P('dp', 'mp'), may hold values from -6 to 6
- loss_token_mask: int32 [32768], P('dp'), may hold values 0 or 1
- adapter_down_weight: bfloat16 [128, 4096], P(None, 'mp'), may hold values from -0.09375 to 0.09375
- adapter_up_weight: bfloat16 [4096, 128], P('mp'), may hold values from -0.5 to 0.5
- width_projection: bfloat16 [2, 4096, 256], P(None, 'mp'), may hold values from -0.09375 to 0.09375
- rank_projection: bfloat16 [2, 128, 16], replicated, may hold values from -0.5 to 0.5
- targets: float32 [64, 8192], P(None, ('dp', 'mp')), may hold values from -500 to 500
Outputs:
- scores: float32 [128, 64], P('dp')
All inputs are finite; a program needn't handle non-finite values. No bound on the sum of `loss_token_mask` on one device may be relied on, other than what follows from the above.
Results may differ from a plain program's by a relative error of at most 0.0003.
Values sent between devices are 32-bit elements; how exact they have to be, the bound alone decides.
A program may use at most 64 MiB of HBM per device.

v0:
```python
import math
import jax
import jax.numpy as jnp
from jax import lax
from jax.sharding import PartitionSpec as P

SEQ = 256
KP = 256
KQ = 16
FEAT = 8192
adapter_scale = 4.0
epsilon = 1e-06


def on_device(
    inputs,
    cotangents,
    loss_token_mask,
    adapter_down_weight,
    adapter_up_weight,
    width_projection,
    rank_projection,
    targets,
):
    samples = inputs.shape[0] // SEQ
    masked_gradient = cotangents * loss_token_mask.astype(jnp.bfloat16)[:, None]
    cols_first = rank_projection[0].astype(jnp.float32)
    cols_second = rank_projection[1].astype(jnp.float32)
    down_partial_gradient = jnp.dot(
        inputs, adapter_down_weight.T, preferred_element_type=jnp.float32
    )
    up_partial_gradient = jnp.dot(
        masked_gradient, adapter_up_weight, preferred_element_type=jnp.float32
    )
    down_rank_product, up_rank_product = lax.psum(
        (down_partial_gradient, up_partial_gradient), "mp"
    )
    compact_up_gradient = jnp.dot(up_rank_product, cols_first, precision=lax.Precision.HIGHEST)
    compact_down_gradient = jnp.dot(down_rank_product, cols_second, precision=lax.Precision.HIGHEST)
    projected_activations = jnp.dot(
        inputs, width_projection[0], preferred_element_type=jnp.float32
    ).reshape(samples, SEQ, KP)
    projected_masked_gradient = jnp.dot(
        masked_gradient, width_projection[1], preferred_element_type=jnp.float32
    ).reshape(samples, SEQ, KP)
    first_matrix = adapter_scale * jnp.einsum(
        "stk,stq->skq",
        projected_activations,
        compact_up_gradient.reshape(samples, SEQ, KQ),
        precision=lax.Precision.HIGHEST,
    )
    second_matrix = adapter_scale * jnp.einsum(
        "stk,stq->skq",
        projected_masked_gradient,
        compact_down_gradient.reshape(samples, SEQ, KQ),
        precision=lax.Precision.HIGHEST,
    )
    partial_value = jnp.concatenate(
        [first_matrix.reshape(samples, KP * KQ), second_matrix.reshape(samples, KP * KQ)], axis=1
    )
    features = lax.psum(partial_value, "mp")
    every_target = lax.all_gather(targets, ("dp", "mp"), axis=1, tiled=True)
    inner = jnp.dot(features, every_target.T, precision=lax.Precision.HIGHEST)
    sample_squares = jnp.sum(features * features, axis=1)
    target_squares = jnp.sum(every_target * every_target, axis=1)
    sample_rms = jnp.sqrt(sample_squares / FEAT + epsilon)
    target_rms = jnp.sqrt(target_squares / FEAT + epsilon)
    return inner / (math.sqrt(FEAT) * sample_rms[:, None] * target_rms[None, :])


def solution(mesh):
    in_specs = (
        P("dp", "mp"),
        P("dp", "mp"),
        P("dp"),
        P(None, "mp"),
        P("mp", None),
        P(None, "mp", None),
        P(),
        P(None, ("dp", "mp")),
    )
    out_specs = P("dp", None)
    return jax.shard_map(
        on_device, mesh=mesh, in_specs=in_specs, out_specs=out_specs, check_vma=False
    )
```

profile of v0, /device:TPU:0, one launch (start us, length us, event | category | flops | bytes accessed | tf_op | source)
XLA Modules:
  0.0 130.8 jit_solution(16499203396642434931)
XLA Ops:
  7.4 0.8 convert_element_type.2
  8.1 7.2 %broadcast_multiply_fusion = bf16[2048,2048]{1,0:T(8,128)(2,1)} fusion(bf16[2048,2048]{1,0:T(8,128)(2,1)} %param.9, bf16[2048]{0:T(1024)(128)(2,1)S(1)} %convert_element_type.2), kind=kLoop, calls=%fused_computation | loop fusion | flops 4194304 | bytes 16781312 | tf_op jit(solution)/shard_map/mul | solution.py:26
  15.4 6.9 %fusion.13 = f32[2048,128]{1,0:T(8,128)} fusion(bf16[2048,2048]{1,0:T(8,128)(2,1)} %param.8, bf16[128,2048]{1,0:T(8,128)(2,1)S(1)} %copy-done), kind=kOutput, calls=%fused_computation.22 | convolution fusion | flops 1073741824 | bytes 9961472 | tf_op jit(solution)/shard_map/dot_general | solution.py:29
  22.3 3.4 %fusion.12 = f32[2048,128]{1,0:T(8,128)} fusion(bf16[2048,2048]{1,0:T(8,128)(2,1)S(1)} %copy-done.1, bf16[2048,128]{1,0:T(8,128)(2,1)S(1)} %copy-done.7), kind=kOutput, calls=%fused_computation.21 | convolution fusion | flops 1073741824 | bytes 9961472 | tf_op jit(solution)/shard_map/dot_general | solution.py:32
  25.7 0.2 all-reduce.4.cloned.1.call-start
  25.9 6.1 %fusion = f32[8,256,256]{2,1,0:T(8,128)S(1)} fusion(bf16[8,256,2048]{2,1,0:T(8,128)(2,1)} %bitcast.34, bf16[2,2048,256]{2,1,0:T(8,128)(2,1)} %param.13), kind=kOutput, calls=%fused_computation.5 | convolution fusion | flops 2147483648 | bytes 11534336 | tf_op jit(solution)/shard_map/dot_general | solution.py:43
  32.1 7.8 %fusion.2 = f32[8,256,256]{2,1,0:T(8,128)} fusion(bf16[8,256,2048]{2,1,0:T(8,128)(2,1)} %bitcast.37, bf16[2,2048,256]{2,1,0:T(8,128)(2,1)S(1)} %copy-done.6), kind=kOutput, calls=%fused_computation.7 | convolution fusion | flops 2147483648 | bytes 11534336 | tf_op jit(solution)/shard_map/dot_general | solution.py:40
  39.9 10.0 %all-reduce.6.cloned.1.call-done = (f32[8,256,128]{2,1,0:T(8,128)}, f32[8,256,128]{2,1,0:T(8,128)}) async-done(((f32[8,256,128]{2,1,0:T(8,128)}, f32[8,256,128]{2,1,0:T(8,128)}), (f32[8,256,128]{2,1,0:T(8,128)}, f32[8,256,128]{2,1,0:T(8,128)})) %all-reduce.6.cloned.1.call-update) | async-done | bytes 2097168 | tf_op jit(solution)/shard_map/psum | solution.py:35
  49.8 1.8 %fusion.6 = f32[8,256,16]{1,2,0:T(8,128)S(1)} fusion(f32[8,256,128]{2,1,0:T(8,128)} %get-tuple-element.5, bf16[2,128,16]{1,2,0:T(8,128)(2,1)S(1)} %copy-done.5), kind=kOutput, calls=%fused_computation.13 | convolution fusion | flops 50331648 | bytes 1183744 | tf_op jit(solution)/shard_map/dot_general | solution.py:39
  51.6 1.2 convolution_multiply_fusion
  52.9 0.3 copy.10
  53.2 0.6 reshape.28
  53.8 0.3 copy-done.4
  54.1 0.6 fusion.8
  54.7 2.8 %convolution_multiply_fusion.1 = f32[8,256,16]{1,2,0:T(8,128)S(1)} fusion(f32[8,256,256]{2,1,0:T(8,128)} %fusion.2, f32[8,256,16]{1,2,0:T(8,128)S(1)} %fusion.8), kind=kOutput, calls=%fused_computation.3 | convolution fusion | flops 100696064 | bytes 2359296 | tf_op jit(solution)/shard_map/stk,stq->skq/dot_general | solution.py:46
  57.5 0.3 copy.9
  57.8 0.6 reshape.27
  58.4 0.7 pad_maximum_fusion
  59.2 0.5 all-gather.2.cloned.1.call-update
  59.8 19.0 %all-reduce.4.cloned.1.call-done = f32[8,8192]{1,0:T(8,128)} async-done(((f32[8,8192]{1,0:T(8,128)}), f32[8,8192]{1,0:T(8,128)}) %all-reduce.4.cloned.1.call-update) | async-done | bytes 262160 | tf_op jit(solution)/shard_map/psum | solution.py:61
  78.8 1.2 multiply_reduce_fusion.1
  80.0 38.8 %all-gather.2.cloned.1.call-done = f32[64,8192]{1,0:T(8,128)} async-done(((f32[64,256]{1,0:T(8,128)}), f32[64,8192]{1,0:T(8,128)}) %all-gather.2.cloned.1.call-update) | async-done | bytes 2097168 | tf_op jit(solution)/shard_map/all_gather | solution.py:62
  118.8 2.0 %multiply_reduce_fusion = f32[64]{0:T(128)S(1)} fusion(f32[64,8192]{1,0:T(8,128)} %all-gather.2.cloned.1.call-done), kind=kLoop, calls=%fused_computation.1 | loop fusion | flops 1048512 | bytes 2097408 | tf_op jit(solution)/shard_map/reduce_sum | solution.py:65
  121.0 2.3 %convolution_divide_fusion = f32[8,64]{1,0:T(8,128)} fusion(f32[8,8192]{1,0:T(8,128)S(1)} %copy-done.3, f32[64,8192]{1,0:T(8,128)S(1)} %copy-done.2, f32[64]{0:T(128)S(1)} %add_sqrt_fusion, f32[8]{0:T(128)S(1)} %sqrt_multiply_fusion), kind=kOutput, calls=%fused_computation.4 | convolution fusion | flops 50332672 | bytes 2361632 | tf_op jit(solution)/shard_map/dot_general | solution.py:63
  (21 shorter events, 0.3 us)
Async XLA Ops:
  7.4 8.0 %copy-start = (bf16[128,2048]{1,0:T(8,128)(2,1)S(1)}, bf16[128,2048]{1,0:T(8,128)(2,1)}, u32[]{:S(2)}) copy-start(bf16[128,2048]{1,0:T(8,128)(2,1)} %param.11) | copy-start | bytes 1572868
  7.4 42.5 %all-reduce.6.cloned.1.call-start = ((), (), s32[]{:S(2)}) async-start(), calls=%async_computation.2 | async-start | bytes 4194304 | tf_op jit(solution)/shard_map/psum | solution.py:35
  15.4 6.9 %copy-start.1 = (bf16[2048,2048]{1,0:T(8,128)(2,1)S(1)}, bf16[2048,2048]{1,0:T(8,128)(2,1)}, u32[]{:S(2)}) copy-start(bf16[2048,2048]{1,0:T(8,128)(2,1)} %broadcast_multiply_fusion) | copy-start | bytes 25165828
  15.4 6.9 %copy-start.7 = (bf16[2048,128]{1,0:T(8,128)(2,1)S(1)}, bf16[2048,128]{1,0:T(8,128)(2,1)}, u32[]{:S(2)}) copy-start(bf16[2048,128]{1,0:T(8,128)(2,1)} %param.12) | copy-start | bytes 1572868
  25.7 53.1 %all-reduce.4.cloned.1.call-start = ((), (), s32[]{:S(2)}) async-start(), calls=%async_computation | async-start | bytes 524288 | tf_op jit(solution)/shard_map/psum | solution.py:61
  25.9 6.1 %copy-start.6 = (bf16[2,2048,256]{2,1,0:T(8,128)(2,1)S(1)}, bf16[2,2048,256]{2,1,0:T(8,128)(2,1)}, u32[]{:S(2)}) copy-start(bf16[2,2048,256]{2,1,0:T(8,128)(2,1)} %param.13) | copy-start | bytes 6291460
  32.1 17.8 %copy-start.5 = (bf16[2,128,16]{1,2,0:T(8,128)(2,1)S(1)}, bf16[2,128,16]{1,2,0:T(8,128)(2,1)}, u32[]{:S(2)}) copy-start(bf16[2,128,16]{1,2,0:T(8,128)(2,1)} %param.14) | copy-start | bytes 24580
  52.8 1.2 copy-start.4
  59.2 59.6 %all-gather.2.cloned.1.call-start = ((), (), s32[]{:S(2)}) async-start(), calls=%async_computation.1 | async-start | bytes 2162688 | tf_op jit(solution)/shard_map/all_gather | solution.py:62
  78.8 42.0 %copy-start.3 = (f32[8,8192]{1,0:T(8,128)S(1)}, f32[8,8192]{1,0:T(8,128)}, u32[]{:S(2)}) copy-start(f32[8,8192]{1,0:T(8,128)} %all-reduce.4.cloned.1.call-done) | copy-start | bytes 786436
  118.8 2.2 %copy-start.2 = (f32[64,8192]{1,0:T(8,128)S(1)}, f32[64,8192]{1,0:T(8,128)}, u32[]{:S(2)}) copy-start(f32[64,8192]{1,0:T(8,128)} %all-gather.2.cloned.1.call-done) | copy-start | bytes 6291460
Sparse Core Ops, SparseCore 0:
  25.8 23.9 all-reduce.5
  59.3 19.4 all-reduce.3
Sparse Core Ops, SparseCore 1:
  62.6 56.1 all-gather.1
where the time goes:
time: 131 us
  waiting for transfers between devices  68.3 us (52%)
  matrix products  32.9 us (25%)
  between operations  14.9 us (11%)
  other arithmetic  11.9 us (9%)
  local copies, waits for them, and re-layouts  2.42 us (2%)
    all_gather x1, waiting for transfers between devices, on_device(): every_target = lax.all_gather(targets, ('dp', 'mp'), axis=1, tiled=True)  38.8 us
    psum x1, waiting for transfers between devices, on_device(): features = lax.psum(partial_value, 'mp')  19 us
    psum x1, waiting for transfers between devices, on_device(): lax.psum((down_partial_gradient, up_partial_gradient), 'mp')  9.98 us
    dot_general x1, matrix products, on_device(): jnp.dot(inputs, width_projection[0], preferred_element_type=jnp.float32)  7.79 us
    mul x1, other arithmetic, on_device(): masked_gradient = cotangents * loss_token_mask.astype(jnp.bfloat16)[:, None]  7.23 us
    dot_general x1, matrix products, on_device(): jnp.dot(inputs, adapter_down_weight.T, preferred_element_type=jnp.float32)  6.87 us
    dot_general x1, matrix products, on_device(): jnp.dot(masked_gradient, width_projection[1], preferred_element_type=jnp....  6.11 us
    dot_general x1, matrix products, on_device(): jnp.dot(masked_gradient, adapter_up_weight, preferred_element_type=jnp.fl...  3.41 us
  transfers between devices with their start and end apart: 3, of which 3 were waited for; matrix products, arithmetic and copies ran while one was open for 12% of the time, Pallas kernels for 0%

commit v1 on v0

--- a/solution.py
+++ b/solution.py
@@ -58,7 +58,7 @@
     partial_value = jnp.concatenate(
         [first_matrix.reshape(samples, KP * KQ), second_matrix.reshape(samples, KP * KQ)], axis=1
     )
-    features = lax.psum(partial_value, "mp")
+    features = jnp.sum(lax.all_gather(partial_value, "mp"), axis=0)
     every_target = lax.all_gather(targets, ("dp", "mp"), axis=1, tiled=True)
     inner = jnp.dot(features, every_target.T, precision=lax.Precision.HIGHEST)
     sample_squares = jnp.sum(features * features, axis=1)

time: 131 us -> 99.5 us (0.76)
  waiting for transfers between devices: 68.3 us -> 36.3 us
  blocking collectives: 0 us -> 2.18 us
  other arithmetic: 11.9 us -> 10.2 us
    psum x1 -> x0, waiting for transfers between devices: 19 us -> none  [on_device(): features = lax.psum(partial_value, 'mp')]
    all_gather x1, waiting for transfers between devices: 38.8 us -> 26.3 us  [on_device(): every_target = lax.all_gather(targets, ('dp', 'mp'), axis=1, tiled=True)]
    all_gather x0 -> x1, blocking collectives: none -> 2.18 us  [on_device(): features = jnp.sum(lax.all_gather(partial_value, 'mp'), axis=0)]
  transfers between devices with their start and end apart: 3 -> 2, of which waited for: 3 -> 2; matrix products, arithmetic and copies ran while one was open for 12% -> 23% of each run, Pallas kernels for 0% -> 0%
where the time goes in v1:
time: 99.5 us; the launch traced here: 99.2 us
  waiting for transfers between devices  36.3 us (36%)
  matrix products  32.9 us (33%)
  between operations  14.9 us (15%)
  other arithmetic  10.2 us (10%)
  local copies, waits for them, and re-layouts  2.43 us (2%)
  blocking collectives  2.18 us (2%)
    all_gather x1, waiting for transfers between devices, on_device(): every_target = lax.all_gather(targets, ('dp', 'mp'), axis=1, tiled=True)  26.3 us
    psum x1, waiting for transfers between devices, on_device(): lax.psum((down_partial_gradient, up_partial_gradient), 'mp')  9.64 us
    dot_general x1, matrix products, on_device(): jnp.dot(inputs, width_projection[0], preferred_element_type=jnp.float32)  7.78 us
    mul x1, other arithmetic, on_device(): masked_gradient = cotangents * loss_token_mask.astype(jnp.bfloat16)[:, None]  7.22 us
    dot_general x1, matrix products, on_device(): jnp.dot(inputs, adapter_down_weight.T, preferred_element_type=jnp.float32)  6.93 us
    dot_general x1, matrix products, on_device(): jnp.dot(masked_gradient, width_projection[1], preferred_element_type=jnp....  6.11 us
    dot_general x1, matrix products, on_device(): jnp.dot(masked_gradient, adapter_up_weight, preferred_element_type=jnp.fl...  3.38 us
    dot_general x1, matrix products, on_device(): jnp.einsum('stk,stq->skq', projected_activations, compact_up_gradient.res...  2.8 us
  transfers between devices with their start and end apart: 2, of which 2 were waited for; matrix products, arithmetic and copies ran while one was open for 23% of the time, Pallas kernels for 0%

profile of v1, /device:TPU:0, one launch (start us, length us, event | category | flops | bytes accessed | tf_op | source)
XLA Modules:
  0.0 99.2 jit_solution(17582928977549881851)
XLA Ops:
  7.4 0.8 convert_element_type.2
  8.1 7.2 %broadcast_multiply_fusion = bf16[2048,2048]{1,0:T(8,128)(2,1)} fusion(bf16[2048,2048]{1,0:T(8,128)(2,1)} %param.9, bf16[2048]{0:T(1024)(128)(2,1)S(1)} %convert_element_type.2), kind=kLoop, calls=%fused_computation | loop fusion | flops 4194304 | bytes 16781312 | tf_op jit(solution)/shard_map/mul | solution.py:26
  15.4 6.9 %fusion.13 = f32[2048,128]{1,0:T(8,128)} fusion(bf16[2048,2048]{1,0:T(8,128)(2,1)} %param.8, bf16[128,2048]{1,0:T(8,128)(2,1)S(1)} %copy-done), kind=kOutput, calls=%fused_computation.23 | convolution fusion | flops 1073741824 | bytes 9961472 | tf_op jit(solution)/shard_map/dot_general | solution.py:29
  22.3 3.4 %fusion.12 = f32[2048,128]{1,0:T(8,128)} fusion(bf16[2048,2048]{1,0:T(8,128)(2,1)S(1)} %copy-done.1, bf16[2048,128]{1,0:T(8,128)(2,1)S(1)} %copy-done.6), kind=kOutput, calls=%fused_computation.22 | convolution fusion | flops 1073741824 | bytes 9961472 | tf_op jit(solution)/shard_map/dot_general | solution.py:32
  25.7 0.2 all-gather.3.cloned.1.call-start
  25.9 0.3 all-gather.3.cloned.1.call-update
  26.3 6.1 %fusion = f32[8,256,256]{2,1,0:T(8,128)S(1)} fusion(bf16[8,256,2048]{2,1,0:T(8,128)(2,1)} %bitcast.36, bf16[2,2048,256]{2,1,0:T(8,128)(2,1)} %param.13), kind=kOutput, calls=%fused_computation.5 | convolution fusion | flops 2147483648 | bytes 11534336 | tf_op jit(solution)/shard_map/dot_general | solution.py:43
  32.4 7.8 %fusion.2 = f32[8,256,256]{2,1,0:T(8,128)} fusion(bf16[8,256,2048]{2,1,0:T(8,128)(2,1)} %bitcast.39, bf16[2,2048,256]{2,1,0:T(8,128)(2,1)S(1)} %copy-done.5), kind=kOutput, calls=%fused_computation.7 | convolution fusion | flops 2147483648 | bytes 11534336 | tf_op jit(solution)/shard_map/dot_general | solution.py:40
  40.2 9.6 %all-reduce.3.cloned.1.call-done = (f32[8,256,128]{2,1,0:T(8,128)}, f32[8,256,128]{2,1,0:T(8,128)}) async-done(((f32[8,256,128]{2,1,0:T(8,128)}, f32[8,256,128]{2,1,0:T(8,128)}), (f32[8,256,128]{2,1,0:T(8,128)}, f32[8,256,128]{2,1,0:T(8,128)})) %all-reduce.3.cloned.1.call-update) | async-done | bytes 2097168 | tf_op jit(solution)/shard_map/psum | solution.py:35
  49.8 1.8 %fusion.6 = f32[8,256,16]{1,2,0:T(8,128)S(1)} fusion(f32[8,256,128]{2,1,0:T(8,128)} %get-tuple-element.5, bf16[2,128,16]{1,2,0:T(8,128)(2,1)S(1)} %copy-done.4), kind=kOutput, calls=%fused_computation.14 | convolution fusion | flops 50331648 | bytes 1183744 | tf_op jit(solution)/shard_map/dot_general | solution.py:39
  51.6 1.2 %convolution_multiply_fusion = f32[8,256,16]{1,2,0:T(8,128)S(1)} fusion(f32[8,256,256]{2,1,0:T(8,128)S(1)} %fusion, f32[8,256,16]{1,2,0:T(8,128)S(1)} %fusion.6), kind=kOutput, calls=%fused_computation.2 | convolution fusion | flops 100696064 | bytes 2359296 | tf_op jit(solution)/shard_map/stk,stq->skq/dot_general | solution.py:52
  52.9 0.3 copy.12
  53.2 0.6 reshape.28
  53.8 0.3 copy-done.3
  54.1 0.6 fusion.8
  54.7 2.8 %convolution_multiply_fusion.1 = f32[8,256,16]{1,2,0:T(8,128)S(1)} fusion(f32[8,256,256]{2,1,0:T(8,128)} %fusion.2, f32[8,256,16]{1,2,0:T(8,128)S(1)} %fusion.8), kind=kOutput, calls=%fused_computation.3 | convolution fusion | flops 100696064 | bytes 2359296 | tf_op jit(solution)/shard_map/stk,stq->skq/dot_general | solution.py:46
  57.5 0.3 copy.11
  57.8 0.6 reshape.27
  58.5 2.2 %all-gather = f32[16,8192]{1,0:T(8,128)S(1)} all-gather(f32[8,8192]{1,0:T(8,128)S(1)} %pad_maximum_fusion), channel_id=2, replica_groups=mesh['dp'=16,'mp'=2] {'mp'}, dimensions={0}, use_global_device_ids=true | all-gather | bytes 786432 | tf_op jit(solution)/shard_map/all_gather | solution.py:61
  60.7 0.2 multiply_reduce_fusion.1
  60.9 26.3 %all-gather.3.cloned.1.call-done = f32[64,8192]{1,0:T(8,128)} async-done(((f32[64,256]{1,0:T(8,128)}), f32[64,8192]{1,0:T(8,128)}) %all-gather.3.cloned.1.call-update) | async-done | bytes 2097168 | tf_op jit(solution)/shard_map/all_gather | solution.py:62
  87.2 2.0 %multiply_reduce_fusion = f32[64]{0:T(128)S(1)} fusion(f32[64,8192]{1,0:T(8,128)} %all-gather.3.cloned.1.call-done), kind=kLoop, calls=%fused_computation.1 | loop fusion | flops 1048512 | bytes 2097408 | tf_op jit(solution)/shard_map/reduce_sum | solution.py:65
  89.2 0.2 copy-done.2
  89.4 2.3 %convolution_divide_fusion = f32[8,64]{1,0:T(8,128)} fusion(f32[8,8192]{1,0:T(8,128)S(1)} %bitcast_reduce_fusion, f32[64,8192]{1,0:T(8,128)S(1)} %copy-done.2, f32[64]{0:T(128)S(1)} %add_sqrt_fusion, f32[8]{0:T(128)S(1)} %sqrt_multiply_fusion), kind=kOutput, calls=%fused_computation.4 | convolution fusion | flops 50332672 | bytes 2361632 | tf_op jit(solution)/shard_map/dot_general | solution.py:63
  (18 shorter events, 0.1 us)
Async XLA Ops:
  7.4 8.0 %copy-start = (bf16[128,2048]{1,0:T(8,128)(2,1)S(1)}, bf16[128,2048]{1,0:T(8,128)(2,1)}, u32[]{:S(2)}) copy-start(bf16[128,2048]{1,0:T(8,128)(2,1)} %param.11) | copy-start | bytes 1572868
  7.4 42.5 %all-reduce.3.cloned.1.call-start = ((), (), s32[]{:S(2)}) async-start(), calls=%async_computation.1 | async-start | bytes 4194304 | tf_op jit(solution)/shard_map/psum | solution.py:35
  15.3 6.9 %copy-start.1 = (bf16[2048,2048]{1,0:T(8,128)(2,1)S(1)}, bf16[2048,2048]{1,0:T(8,128)(2,1)}, u32[]{:S(2)}) copy-start(bf16[2048,2048]{1,0:T(8,128)(2,1)} %broadcast_multiply_fusion) | copy-start | bytes 25165828
  15.4 6.9 %copy-start.6 = (bf16[2048,128]{1,0:T(8,128)(2,1)S(1)}, bf16[2048,128]{1,0:T(8,128)(2,1)}, u32[]{:S(2)}) copy-start(bf16[2048,128]{1,0:T(8,128)(2,1)} %param.12) | copy-start | bytes 1572868
  25.7 61.5 %all-gather.3.cloned.1.call-start = ((), (), s32[]{:S(2)}) async-start(), calls=%async_computation | async-start | bytes 2162688 | tf_op jit(solution)/shard_map/all_gather | solution.py:62
  26.3 6.1 %copy-start.5 = (bf16[2,2048,256]{2,1,0:T(8,128)(2,1)S(1)}, bf16[2,2048,256]{2,1,0:T(8,128)(2,1)}, u32[]{:S(2)}) copy-start(bf16[2,2048,256]{2,1,0:T(8,128)(2,1)} %param.13) | copy-start | bytes 6291460
  32.4 17.4 %copy-start.4 = (bf16[2,128,16]{1,2,0:T(8,128)(2,1)S(1)}, bf16[2,128,16]{1,2,0:T(8,128)(2,1)}, u32[]{:S(2)}) copy-start(bf16[2,128,16]{1,2,0:T(8,128)(2,1)} %param.14) | copy-start | bytes 24580
  52.9 1.2 %copy-start.3 = (f32[8,256,128]{2,1,0:T(8,128)S(1)}, f32[8,256,128]{2,1,0:T(8,128)}, u32[]{:S(2)}) copy-start(f32[8,256,128]{2,1,0:T(8,128)} %get-tuple-element.6) | copy-start | bytes 3145732
  87.2 2.2 %copy-start.2 = (f32[64,8192]{1,0:T(8,128)S(1)}, f32[64,8192]{1,0:T(8,128)}, u32[]{:S(2)}) copy-start(f32[64,8192]{1,0:T(8,128)} %all-gather.3.cloned.1.call-done) | copy-start | bytes 6291460
Sparse Core Ops, SparseCore 0:
  25.8 23.9 all-reduce.2
Sparse Core Ops, SparseCore 1:
  29.5 57.7 all-gather.2
